TPU v7x, 32 devices: a whole 2x2x4 slice. The times are simulated.
32 devices in a mesh: groups: 2 (over y), row: 4 (over z), col: 4 (over x, core).
Axes of the slice: x: 2, y: 2, z: 4, core: 2. Of those that a mesh axis runs over, the one named last changes fastest.
Arguments:
- queries: bfloat16 [4096, 1024], P(('groups', 'row'), 'col'), parts along dimension 0, may hold values from -64 to 64
- keys: bfloat16 [4096, 1024], P(('groups', 'col'), 'row'), parts along dimension 0, may hold values from -6 to 6
- values: bfloat16 [4096, 1024], P(('groups', 'col'), 'row'), parts along dimension 0, may hold values from -6 to 6
- cotangent: bfloat16 [4096, 1024], P(('groups', 'row'), 'col'), parts along dimension 0, may hold values from -6 to 6
- block_lists: int32 [32, 16], P(('groups', 'row')), parts along dimension 0, may hold values from 0 to 15, as said below
- block_counts: int32 [32], P(('groups', 'row')), parts along dimension 0, may hold values from 1 to 16, as said below
Outputs:
- attended: bfloat16 [4096, 1024], P(('groups', 'row'), 'col'), parts along dimension 0
- grad_queries: bfloat16 [4096, 1024], P(('groups', 'row'), 'col'), parts along dimension 0
- grad_keys: bfloat16 [4096, 1024], P(('groups', 'col'), 'row'), parts along dimension 0
- grad_values: bfloat16 [4096, 1024], P(('groups', 'col'), 'row'), parts along dimension 0
There are 2 independent parts, one for each index of `groups`. A program takes and returns all parts, laid end to end along the dimension named above; each array names one. Nothing has to cross between parts.
Inputs may be any that keep to these rules, and one draw needn't show every extreme that they name: `block_lists`: each row lists 16 distinct blocks; its first entry is the query block itself. `block_counts`: some query block has all 16 entries live in every draw.
All inputs are finite; a program needn't handle non-finite values.
Results may differ from a plain program's by a relative error of at most 0.011.
Values may be sent and summed in bfloat16 or wider, within the bound.
No kernel may reach another device: no remote copies, remote signals or barrier semaphores. Data moves between devices by JAX's collectives and lax.ppermute only.
A program may use at most 64 MiB of HBM per device.

v0:
```python
import math
import jax
import jax.numpy as jnp
from jax import lax
from jax.sharding import PartitionSpec as P

D = 1024
HEADS = 16
HEAD = 64
BLK = 128
MAXNB = 16
NEG_FILL = -1e30


def tile_scores(query_tile, key_tile, score_scale):
    query_heads = query_tile.reshape(query_tile.shape[0], HEADS, -1)
    key_heads = key_tile.reshape(key_tile.shape[0], HEADS, -1)
    return (
        jnp.einsum("qhd,khd->hqk", query_heads, key_heads, preferred_element_type=jnp.float32)
        * score_scale
    )


def on_device(queries, keys, values, cotangent, block_lists, block_counts):
    score_scale = 1.0 / math.sqrt(HEAD)
    q_full = lax.all_gather(queries, "col", axis=1, tiled=True)
    k_full, v_full = (
        lax.all_gather(keys, "row", axis=1, tiled=True),
        lax.all_gather(values, "row", axis=1, tiled=True),
    )
    q_rows = q_full.shape[0]
    k_rows = k_full.shape[0]
    q_blocks = q_rows // BLK
    k_blocks = k_rows // BLK
    group_size = min(4, q_blocks)
    span_rows = group_size * BLK
    supers = q_blocks // group_size
    tile_count = supers * k_blocks
    first_key = lax.axis_index("col") * k_blocks
    wanted = first_key + jnp.arange(k_blocks, dtype=jnp.int32)
    live_slots = jnp.arange(MAXNB, dtype=jnp.int32)[None, :] < block_counts[:, None]
    block_hit = jnp.any(
        (block_lists[:, :, None] == wanted[None, None, :]) & live_slots[:, :, None], axis=1
    )
    block_hit = block_hit.reshape(supers, group_size, k_blocks).transpose(0, 2, 1)
    row_mask = jnp.repeat(block_hit, BLK, axis=2)
    tile_any = jnp.any(block_hit, axis=2)

    def tile_parts(step):
        super_at = step // k_blocks
        key_at = step % k_blocks
        query_tile = lax.dynamic_slice_in_dim(q_full, super_at * span_rows, span_rows, 0)
        key_tile = lax.dynamic_slice_in_dim(k_full, key_at * BLK, BLK, 0)
        value_tile = lax.dynamic_slice_in_dim(v_full, key_at * BLK, BLK, 0)
        keep_mask = row_mask[super_at, key_at][None, :, None]
        return (super_at, key_at, query_tile, key_tile, value_tile, keep_mask)

    def unchanged(carry):
        return carry

    def stats_step(step, carry):
        super_at, key_at, query_tile, key_tile, value_tile, keep_mask = tile_parts(step)

        def stats_work(state):
            row_top, row_total = state
            scores = jnp.where(keep_mask, tile_scores(query_tile, key_tile, score_scale), NEG_FILL)
            old_top = lax.dynamic_slice_in_dim(row_top, super_at * span_rows, span_rows, 1)
            old_total = lax.dynamic_slice_in_dim(row_total, super_at * span_rows, span_rows, 1)
            new_top = jnp.maximum(old_top, jnp.max(scores, axis=2))
            exp_terms = jnp.where(keep_mask, jnp.exp(scores - new_top[:, :, None]), 0.0)
            fresh = old_total * jnp.exp(old_top - new_top) + jnp.sum(exp_terms, axis=2)
            return (
                lax.dynamic_update_slice_in_dim(row_top, new_top, super_at * span_rows, 1),
                lax.dynamic_update_slice_in_dim(row_total, fresh, super_at * span_rows, 1),
            )

        return lax.cond(tile_any[super_at, key_at], stats_work, unchanged, carry)

    start_top = jnp.full((HEADS, q_rows), NEG_FILL, jnp.float32)
    start_total = jnp.zeros((HEADS, q_rows), jnp.float32)
    local_top, local_total = lax.fori_loop(0, tile_count, stats_step, (start_top, start_total))
    row_top = lax.pmax(local_top.astype(jnp.bfloat16), "col").astype(local_top.dtype)
    row_total = lax.psum(local_total * jnp.exp(local_top - row_top), "col")

    def tile_weights(scores, super_at, keep_mask):
        top_rows = lax.dynamic_slice_in_dim(row_top, super_at * span_rows, span_rows, 1)
        total_rows = lax.dynamic_slice_in_dim(row_total, super_at * span_rows, span_rows, 1)
        ratio = jnp.exp(scores - top_rows[:, :, None]) / total_rows[:, :, None]
        return jnp.where(keep_mask, ratio, 0.0).astype(jnp.bfloat16)

    def output_step(step, carry):
        super_at, key_at, query_tile, key_tile, value_tile, keep_mask = tile_parts(step)

        def output_work(out_rows):
            scores = jnp.where(keep_mask, tile_scores(query_tile, key_tile, score_scale), NEG_FILL)
            weights = tile_weights(scores, super_at, keep_mask)
            value_heads = value_tile.reshape(BLK, HEADS, -1)
            part = jnp.einsum(
                "hqk,khd->qhd", weights, value_heads, preferred_element_type=jnp.float32
            ).reshape(span_rows, -1)
            current = lax.dynamic_slice_in_dim(out_rows, super_at * span_rows, span_rows, 0)
            return lax.dynamic_update_slice_in_dim(
                out_rows, current + part, super_at * span_rows, 0
            )

        return lax.cond(tile_any[super_at, key_at], output_work, unchanged, carry)

    partial_out = lax.fori_loop(0, tile_count, output_step, jnp.zeros((q_rows, D), jnp.float32))
    out_share = lax.psum_scatter(partial_out, "col", scatter_dimension=1, tiled=True).astype(
        jnp.bfloat16
    )
    grad_full, out_full = (
        lax.all_gather(cotangent, "col", axis=1, tiled=True),
        lax.all_gather(out_share, "col", axis=1, tiled=True),
    )
    delta = jnp.einsum(
        "qhd,qhd->hq",
        grad_full.reshape(q_rows, HEADS, -1),
        out_full.reshape(q_rows, HEADS, -1),
        preferred_element_type=jnp.float32,
    )

    def grad_step(step, carry):
        super_at, key_at, query_tile, key_tile, value_tile, keep_mask = tile_parts(step)

        def grad_work(state):
            query_accum, key_accum, value_accum = state
            scores = jnp.where(keep_mask, tile_scores(query_tile, key_tile, score_scale), NEG_FILL)
            weights = tile_weights(scores, super_at, keep_mask)
            grad_tile = lax.dynamic_slice_in_dim(
                grad_full, super_at * span_rows, span_rows, 0
            ).reshape(span_rows, HEADS, -1)
            value_heads = value_tile.reshape(BLK, HEADS, -1)
            key_heads = key_tile.reshape(BLK, HEADS, -1)
            query_heads = query_tile.reshape(span_rows, HEADS, -1)
            dweights = jnp.einsum(
                "qhd,khd->hqk", grad_tile, value_heads, preferred_element_type=jnp.float32
            )
            delta_rows = lax.dynamic_slice_in_dim(delta, super_at * span_rows, span_rows, 1)
            dscores = (weights.astype(jnp.float32) * (dweights - delta_rows[:, :, None])).astype(
                jnp.bfloat16
            )
            query_part = score_scale * jnp.einsum(
                "hqk,khd->qhd", dscores, key_heads, preferred_element_type=jnp.float32
            )
            key_part = score_scale * jnp.einsum(
                "hqk,qhd->khd", dscores, query_heads, preferred_element_type=jnp.float32
            )
            value_part = jnp.einsum(
                "hqk,qhd->khd", weights, grad_tile, preferred_element_type=jnp.float32
            )
            query_now = lax.dynamic_slice_in_dim(query_accum, super_at * span_rows, span_rows, 0)
            key_now = lax.dynamic_slice_in_dim(key_accum, key_at * BLK, BLK, 0)
            value_now = lax.dynamic_slice_in_dim(value_accum, key_at * BLK, BLK, 0)
            query_accum = lax.dynamic_update_slice_in_dim(
                query_accum, query_now + query_part.reshape(span_rows, -1), super_at * span_rows, 0
            )
            key_accum = lax.dynamic_update_slice_in_dim(
                key_accum, key_now + key_part.reshape(BLK, -1), key_at * BLK, 0
            )
            value_accum = lax.dynamic_update_slice_in_dim(
                value_accum, value_now + value_part.reshape(BLK, -1), key_at * BLK, 0
            )
            return (query_accum, key_accum, value_accum)

        return lax.cond(tile_any[super_at, key_at], grad_work, unchanged, carry)

    start_grads = (
        jnp.zeros((q_rows, D), jnp.float32),
        jnp.zeros((k_rows, D), jnp.float32),
        jnp.zeros((k_rows, D), jnp.float32),
    )
    query_parts, key_parts, value_parts = lax.fori_loop(0, tile_count, grad_step, start_grads)
    grad_queries = lax.psum_scatter(query_parts, "col", scatter_dimension=1, tiled=True).astype(
        jnp.bfloat16
    )
    grad_keys, grad_values = (
        lax.psum_scatter(key_parts, "row", scatter_dimension=1, tiled=True),
        lax.psum_scatter(value_parts, "row", scatter_dimension=1, tiled=True),
    )
    return (
        out_share,
        grad_queries,
        grad_keys.astype(jnp.bfloat16),
        grad_values.astype(jnp.bfloat16),
    )


def solution(mesh):
    return jax.shard_map(
        on_device,
        mesh=mesh,
        in_specs=(
            P(("groups", "row"), "col"),
            P(("groups", "col"), "row"),
            P(("groups", "col"), "row"),
            P(("groups", "row"), "col"),
            P(("groups", "row"), None),
            P(("groups", "row")),
        ),
        out_specs=(
            P(("groups", "row"), "col"),
            P(("groups", "row"), "col"),
            P(("groups", "col"), "row"),
            P(("groups", "col"), "row"),
        ),
        check_vma=False,
    )
```

profile of v0, /device:TPU:0, one launch (start us, length us, event | category | flops | bytes accessed | tf_op | source)
XLA Modules:
  0.0 402.9 jit_solution(14908098541145584658)
XLA Ops:
  13.3 16.3 %all-gather.8.cloned.1.call-done = bf16[512,1024]{0,1:T(8,128)(2,1)} async-done(((bf16[512,256]{0,1:T(8,128)(2,1)}), bf16[512,1024]{0,1:T(8,128)(2,1)}) %all-gather.8.cloned.1.call-update) | async-done | bytes 1048592 | tf_op jit(solution)/shard_map/all_gather | solution.py:26
  29.6 30.1 %all-gather.6.cloned.1.call-done = bf16[512,1024]{0,1:T(8,128)(2,1)} async-done(((bf16[512,256]{0,1:T(8,128)(2,1)}), bf16[512,1024]{0,1:T(8,128)(2,1)}) %all-gather.6.cloned.1.call-update) | async-done | bytes 1048592 | tf_op jit(solution)/shard_map/all_gather | solution.py:28
  59.7 21.9 %while.57 = (s32[]{:T(128)}, f32[16,512]{1,0:T(8,128)S(1)}, f32[16,512]{1,0:T(8,128)S(1)}, pred[1,4]{1,0:T(4,128)(4,1)S(1)}, bf16[512,1024]{0,1:T(8,128)(2,1)}, ...) while((s32[]{:T(128)}, f32[16,512]{1,0:T(8,128)S(1)}, ...), condition=%wide.region_7.8_spmd.clone, body=%wide.region_2.7_spmd.clone.sunk | while | flops 142622736 | bytes 10658168 | solution.py:81
  60.3 4.8 %conditional.9 = ((f32[16,512]{1,0:T(8,128)S(1)}, f32[16,512]{1,0:T(8,128)S(1)})) conditional(s32[]{:T(128)} %bitcast.68, (f32[16,512]{1,0:T(8,128)S(1)}, f32[16,512]{1,0:T(8,128)S(1)}) %tuple.194, (pred[4,4]{1,0:T(4,128)(4,1)S(1)}, s32[]{:T(128)}, s32[]{:T(128)}, bf16[512,1024]{0,1:T(8,128)(2,1)}, bf16[512,1024]{0,1:T(8,128)(2,1)}, ...), branch_computations={%region_3.3_spmd, %region_4.6_spmd} | conditional | flops 142622720 | bytes 10657886 | solution.py:77
  65.8 4.9 %conditional.9 = ((f32[16,512]{1,0:T(8,128)S(1)}, f32[16,512]{1,0:T(8,128)S(1)})) conditional(s32[]{:T(128)} %bitcast.68, (f32[16,512]{1,0:T(8,128)S(1)}, f32[16,512]{1,0:T(8,128)S(1)}) %tuple.194, (pred[4,4]{1,0:T(4,128)(4,1)S(1)}, s32[]{:T(128)}, s32[]{:T(128)}, bf16[512,1024]{0,1:T(8,128)(2,1)}, bf16[512,1024]{0,1:T(8,128)(2,1)}, ...), branch_computations={%region_3.3_spmd, %region_4.6_spmd} | conditional | flops 142622720 | bytes 10657886 | solution.py:77
  71.3 4.8 %conditional.9 = ((f32[16,512]{1,0:T(8,128)S(1)}, f32[16,512]{1,0:T(8,128)S(1)})) conditional(s32[]{:T(128)} %bitcast.68, (f32[16,512]{1,0:T(8,128)S(1)}, f32[16,512]{1,0:T(8,128)S(1)}) %tuple.194, (pred[4,4]{1,0:T(4,128)(4,1)S(1)}, s32[]{:T(128)}, s32[]{:T(128)}, bf16[512,1024]{0,1:T(8,128)(2,1)}, bf16[512,1024]{0,1:T(8,128)(2,1)}, ...), branch_computations={%region_3.3_spmd, %region_4.6_spmd} | conditional | flops 142622720 | bytes 10657886 | solution.py:77
  76.8 4.8 %conditional.9 = ((f32[16,512]{1,0:T(8,128)S(1)}, f32[16,512]{1,0:T(8,128)S(1)})) conditional(s32[]{:T(128)} %bitcast.68, (f32[16,512]{1,0:T(8,128)S(1)}, f32[16,512]{1,0:T(8,128)S(1)}) %tuple.194, (pred[4,4]{1,0:T(4,128)(4,1)S(1)}, s32[]{:T(128)}, s32[]{:T(128)}, bf16[512,1024]{0,1:T(8,128)(2,1)}, bf16[512,1024]{0,1:T(8,128)(2,1)}, ...), branch_computations={%region_3.3_spmd, %region_4.6_spmd} | conditional | flops 142622720 | bytes 10657886 | solution.py:77
  81.6 11.3 %pmax.7 = bf16[16,512]{1,0:T(8,128)(2,1)S(1)} all-reduce(bf16[16,512]{1,0:T(8,128)(2,1)S(1)} %convert_element_type.89), channel_id=1, replica_groups=mesh['groups'=2,'row'=4,'col'=4] {'col'}, use_global_device_ids=true, to_apply=%region_8.9 | all-reduce | flops 8192 | bytes 32768 | tf_op jit(solution)/shard_map/pmax | solution.py:82
  92.9 10.3 %psum.7 = f32[16,512]{1,0:T(8,128)S(1)} all-reduce(f32[16,512]{1,0:T(8,128)S(1)} %exponential_multiply_fusion), channel_id=1, replica_groups=mesh['groups'=2,'row'=4,'col'=4] {'col'}, use_global_device_ids=true, to_apply=%region_9.10 | all-reduce | flops 8192 | bytes 65536 | tf_op jit(solution)/shard_map/psum | solution.py:83
  103.5 36.9 %while.58 = (s32[]{:T(128)}, f32[512,1024]{0,1:T(8,128)S(1)}, pred[1,4]{1,0:T(4,128)(4,1)S(1)}, bf16[512,1024]{0,1:T(8,128)(2,1)}, bf16[512,1024]{0,1:T(8,128)(2...) while((s32[]{:T(128)}, f32[512,1024]{0,1:T(8,128)S(1)}, ...), condition=%wide.region_13.14_spmd.clone, body=%wide.region_10.13_spmd.clone.sunk | while | flops 275251200 | bytes 11083640 | solution.py:108
  104.2 8.6 %conditional.10 = (f32[512,1024]{0,1:T(8,128)S(1)}) conditional(s32[]{:T(128)} %bitcast.69, f32[512,1024]{0,1:T(8,128)S(1)} %get-tuple-element.1617, (pred[4,4]{1,0:T(4,128)(4,1)S(1)}, s32[]{:T(128)}, s32[]{:T(128)}, bf16[512,1024]{0,1:T(8,128)(2,1)}, bf16[512,1024]{0,1:T(8,128)(2,1)S(1)}, /*index=5*/f32[16,512]{1,0:T(8,128)S(1)}, ...), branch_computations={%region_11.11_spmd, %region_12.12_spmd} | conditional | flops 275251200 | bytes 11083342 | solution.py:106
  106.8 3.8 fusion.9
  113.4 8.6 %conditional.10 = (f32[512,1024]{0,1:T(8,128)S(1)}) conditional(s32[]{:T(128)} %bitcast.69, f32[512,1024]{0,1:T(8,128)S(1)} %get-tuple-element.1617, (pred[4,4]{1,0:T(4,128)(4,1)S(1)}, s32[]{:T(128)}, s32[]{:T(128)}, bf16[512,1024]{0,1:T(8,128)(2,1)}, bf16[512,1024]{0,1:T(8,128)(2,1)S(1)}, /*index=5*/f32[16,512]{1,0:T(8,128)S(1)}, ...), branch_computations={%region_11.11_spmd, %region_12.12_spmd} | conditional | flops 275251200 | bytes 11083342 | solution.py:106
  116.0 3.8 fusion.9
  122.6 8.6 %conditional.10 = (f32[512,1024]{0,1:T(8,128)S(1)}) conditional(s32[]{:T(128)} %bitcast.69, f32[512,1024]{0,1:T(8,128)S(1)} %get-tuple-element.1617, (pred[4,4]{1,0:T(4,128)(4,1)S(1)}, s32[]{:T(128)}, s32[]{:T(128)}, bf16[512,1024]{0,1:T(8,128)(2,1)}, bf16[512,1024]{0,1:T(8,128)(2,1)S(1)}, /*index=5*/f32[16,512]{1,0:T(8,128)S(1)}, ...), branch_computations={%region_11.11_spmd, %region_12.12_spmd} | conditional | flops 275251200 | bytes 11083342 | solution.py:106
  125.2 3.8 fusion.9
  131.9 8.6 %conditional.10 = (f32[512,1024]{0,1:T(8,128)S(1)}) conditional(s32[]{:T(128)} %bitcast.69, f32[512,1024]{0,1:T(8,128)S(1)} %get-tuple-element.1617, (pred[4,4]{1,0:T(4,128)(4,1)S(1)}, s32[]{:T(128)}, s32[]{:T(128)}, bf16[512,1024]{0,1:T(8,128)(2,1)}, bf16[512,1024]{0,1:T(8,128)(2,1)S(1)}, /*index=5*/f32[16,512]{1,0:T(8,128)S(1)}, ...), branch_computations={%region_11.11_spmd, %region_12.12_spmd} | conditional | flops 275251200 | bytes 11083342 | solution.py:106
  134.4 3.8 fusion.9
  142.8 29.6 %reduce-scatter.5.cloned.1.call-done = f32[512,256]{0,1:T(8,128)} async-done(((f32[512,1024]{0,1:T(8,128)}), f32[512,256]{0,1:T(8,128)}) %reduce-scatter.5.cloned.1.call-update) | async-done | bytes 524304 | tf_op jit(solution)/shard_map/reduce_scatter | solution.py:109
  174.2 17.0 %all-gather.12.cloned.1.call-done = bf16[512,1024]{0,1:T(8,128)(2,1)} async-done(((bf16[512,256]{0,1:T(8,128)(2,1)}), bf16[512,1024]{0,1:T(8,128)(2,1)}) %all-gather.12.cloned.1.call-update) | async-done | bytes 1048592 | tf_op jit(solution)/shard_map/all_gather | solution.py:113
  191.2 18.8 %all-gather.14.cloned.1.call-done = bf16[512,1024]{0,1:T(8,128)(2,1)} async-done(((bf16[512,256]{0,1:T(8,128)(2,1)}), bf16[512,1024]{0,1:T(8,128)(2,1)}) %all-gather.14.cloned.1.call-update) | async-done | bytes 1048592 | tf_op jit(solution)/shard_map/all_gather | solution.py:114
  216.6 51.4 %while.59 = (s32[]{:T(128)}, f32[512,1024]{0,1:T(8,128)}, f32[512,1024]{0,1:T(8,128)}, f32[512,1024]{0,1:T(8,128)}, pred[1,4]{1,0:T(4,128)(4,1)S(1)}, /*index=5*...) while((s32[]{:T(128)}, f32[512,1024]{0,1:T(8,128)}, ...), condition=%wide.region_18.19_spmd.clone, body=%wide.region_15.18_spmd.clone.sunk | while | flops 683016192 | bytes 48078884 | solution.py:173
  217.2 12.3 %conditional.11 = ((f32[512,1024]{0,1:T(8,128)}, f32[512,1024]{0,1:T(8,128)}, f32[512,1024]{0,1:T(8,128)})) conditional(s32[]{:T(128)} %bitcast.70, (f32[512,1024]{0,1:T(8,128)}, f32[512,1024]{0,1:T(8,128)}, f32[512,1024]{0,1:T(8,128)}) %tuple.199, (pred[4,4]{1,0:T(4,128)(4,1)S(1)}, s32[]{:T(128)}, s32[]{:T(128)}, bf16[512,1024]{0,1:T(8,128)(2,1)}, ...), branch_computations={%region_16.16_spmd, %region_17.17_spmd} | conditional | flops 683016192 | bytes 48078500 | solution.py:166
  230.1 12.3 %conditional.11 = ((f32[512,1024]{0,1:T(8,128)}, f32[512,1024]{0,1:T(8,128)}, f32[512,1024]{0,1:T(8,128)})) conditional(s32[]{:T(128)} %bitcast.70, (f32[512,1024]{0,1:T(8,128)}, f32[512,1024]{0,1:T(8,128)}, f32[512,1024]{0,1:T(8,128)}) %tuple.199, (pred[4,4]{1,0:T(4,128)(4,1)S(1)}, s32[]{:T(128)}, s32[]{:T(128)}, bf16[512,1024]{0,1:T(8,128)(2,1)}, ...), branch_computations={%region_16.16_spmd, %region_17.17_spmd} | conditional | flops 683016192 | bytes 48078500 | solution.py:166
  240.0 2.4 constant_dynamic-update-slice_fusion
  242.9 12.3 %conditional.11 = ((f32[512,1024]{0,1:T(8,128)}, f32[512,1024]{0,1:T(8,128)}, f32[512,1024]{0,1:T(8,128)})) conditional(s32[]{:T(128)} %bitcast.70, (f32[512,1024]{0,1:T(8,128)}, f32[512,1024]{0,1:T(8,128)}, f32[512,1024]{0,1:T(8,128)}) %tuple.199, (pred[4,4]{1,0:T(4,128)(4,1)S(1)}, s32[]{:T(128)}, s32[]{:T(128)}, bf16[512,1024]{0,1:T(8,128)(2,1)}, ...), branch_computations={%region_16.16_spmd, %region_17.17_spmd} | conditional | flops 683016192 | bytes 48078500 | solution.py:166
  255.8 12.3 %conditional.11 = ((f32[512,1024]{0,1:T(8,128)}, f32[512,1024]{0,1:T(8,128)}, f32[512,1024]{0,1:T(8,128)})) conditional(s32[]{:T(128)} %bitcast.70, (f32[512,1024]{0,1:T(8,128)}, f32[512,1024]{0,1:T(8,128)}, f32[512,1024]{0,1:T(8,128)}) %tuple.199, (pred[4,4]{1,0:T(4,128)(4,1)S(1)}, s32[]{:T(128)}, s32[]{:T(128)}, bf16[512,1024]{0,1:T(8,128)(2,1)}, ...), branch_computations={%region_16.16_spmd, %region_17.17_spmd} | conditional | flops 683016192 | bytes 48078500 | solution.py:166
  265.7 2.4 constant_dynamic-update-slice_fusion
  268.1 2.9 copy.37
  279.6 35.4 %reduce-scatter.11.cloned.1.call-done = f32[512,256]{1,0:T(8,128)} async-done(((f32[512,1024]{1,0:T(8,128)}), f32[512,256]{1,0:T(8,128)}) %reduce-scatter.11.cloned.1.call-update) | async-done | bytes 524304 | tf_op jit(solution)/shard_map/reduce_scatter | solution.py:179
  316.8 31.5 %reduce-scatter.7.cloned.1.call-done = f32[512,256]{1,0:T(8,128)} async-done(((f32[512,1024]{1,0:T(8,128)}), f32[512,256]{1,0:T(8,128)}) %reduce-scatter.7.cloned.1.call-update) | async-done | bytes 524304 | tf_op jit(solution)/shard_map/reduce_scatter | solution.py:174
  350.1 44.5 %reduce-scatter.9.cloned.1.call-done = f32[512,256]{1,0:T(8,128)} async-done(((f32[512,1024]{1,0:T(8,128)}), f32[512,256]{1,0:T(8,128)}) %reduce-scatter.9.cloned.1.call-update) | async-done | bytes 524304 | tf_op jit(solution)/shard_map/reduce_scatter | solution.py:178
  (192 shorter events, 112.9 us)
Async XLA Ops:
  7.2 5.7 %copy-start.10 = (s32[4]{0:T(128)S(1)}, s32[4]{0:T(128)}, u32[]{:S(2)}) copy-start(s32[4]{0:T(128)} %param.23) | copy-start | bytes 52
  7.2 5.8 %copy-start.9 = (s32[4,16]{1,0:T(4,128)S(1)}, s32[4,16]{1,0:T(4,128)}, u32[]{:S(2)}) copy-start(s32[4,16]{1,0:T(4,128)} %param.22) | copy-start | bytes 772
  7.2 22.4 %all-gather.8.cloned.1.call-start = ((), (), s32[]{:S(2)}) async-start(), calls=%async_computation.5 | async-start | bytes 1310720 | tf_op jit(solution)/shard_map/all_gather | solution.py:26
  9.1 50.7 %all-gather.6.cloned.1.call-start = ((), (), s32[]{:S(2)}) async-start(), calls=%async_computation.4 | async-start | bytes 1310720 | tf_op jit(solution)/shard_map/all_gather | solution.py:28
  10.9 92.3 %all-gather.10.cloned.1.call-start = ((), (), s32[]{:S(2)}) async-start(), calls=%async_computation.6 | async-start | bytes 1310720 | tf_op jit(solution)/shard_map/all_gather | solution.py:29
  12.8 159.5 %reduce-scatter.5.cloned.1.call-start = ((), (), s32[]{:S(2)}) async-start(), calls=%async_computation.7 | async-start | bytes 2621440 | tf_op jit(solution)/shard_map/reduce_scatter | solution.py:109
  81.6 21.9 %copy-start.1 = (bf16[512,1024]{0,1:T(8,128)(2,1)S(1)}, bf16[512,1024]{0,1:T(8,128)(2,1)}, u32[]{:S(2)}) copy-start(bf16[512,1024]{0,1:T(8,128)(2,1)} %get-tuple-element.1707) | copy-start | bytes 3145732
  140.4 1.3 copy-start.5
  140.4 1.4 copy-start.8
  141.8 49.4 %all-gather.12.cloned.1.call-start = ((), (), s32[]{:S(2)}) async-start(), calls=%async_computation.8 | async-start | bytes 1310720 | tf_op jit(solution)/shard_map/all_gather | solution.py:113
  142.7 67.3 %all-gather.14.cloned.1.call-start = ((), (), s32[]{:S(2)}) async-start(), calls=%async_computation.9 | async-start | bytes 1310720 | tf_op jit(solution)/shard_map/all_gather | solution.py:114
  174.1 140.9 %reduce-scatter.11.cloned.1.call-start = ((), (), s32[]{:S(2)}) async-start(), calls=%async_computation.12 | async-start | bytes 2621440 | tf_op jit(solution)/shard_map/reduce_scatter | solution.py:179
  213.5 3.2 copy-start
  223.7 1.6 copy-start.2
  225.8 1.3 copy-start.3
  236.5 1.6 copy-start.2
  238.7 1.3 copy-start.3
  249.4 1.6 copy-start.2
  251.5 1.3 copy-start.3
  262.2 1.6 copy-start.2
  264.4 1.3 copy-start.3
  271.0 1.6 copy-start.4
  271.0 77.3 %reduce-scatter.7.cloned.1.call-start = ((), (), s32[]{:S(2)}) async-start(), calls=%async_computation.10 | async-start | bytes 2621440 | tf_op jit(solution)/shard_map/reduce_scatter | solution.py:174
  274.4 1.6 copy-start.6
  274.4 120.2 %reduce-scatter.9.cloned.1.call-start = ((), (), s32[]{:S(2)}) async-start(), calls=%async_computation.11 | async-start | bytes 2621440 | tf_op jit(solution)/shard_map/reduce_scatter | solution.py:178
  277.8 0.9 copy-start.7
Sparse Core Ops, SparseCore 0:
  10.2 19.4 all-gather.7
  31.7 27.9 all-gather.5
  61.9 27.4 all-gather.9
  141.9 30.3 reduce-scatter.4
  174.4 16.7 all-gather.11
  193.2 16.7 all-gather.13
  271.1 43.8 reduce-scatter.10
  317.6 30.7 reduce-scatter.6
  350.7 43.8 reduce-scatter.8
where the time goes:
time: 405 us; the launch traced here: 403 us
  waiting for transfers between devices  223 us (55%)
  local copies, waits for them, and re-layouts  54.1 us (13%)
  other arithmetic  41 us (10%)
  matrix products  40.2 us (10%)
  blocking collectives  21.5 us (5%)
  between operations  14 us (3%)
  loops' own time  8.27 us (2%)
    reduce_scatter x1, waiting for transfers between devices, on_device(): lax.psum_scatter(key_parts, 'row', scatter_dimension=1, tiled=True)  44.5 us
    reduce_scatter x1, waiting for transfers between devices, on_device(): lax.psum_scatter(value_parts, 'row', scatter_dimension=1, tiled=True)  35.4 us
    reduce_scatter x1, waiting for transfers between devices, on_device(): lax.psum_scatter(query_parts, 'col', scatter_dimension=1, tiled=True)  31.5 us
    all_gather x1, waiting for transfers between devices, on_device(): lax.all_gather(keys, 'row', axis=1, tiled=True)  30.1 us
    reduce_scatter x1, waiting for transfers between devices, on_device(): lax.psum_scatter(partial_out, 'col', scatter_dimension=1, tiled=True)  29.6 us
    all_gather x1, waiting for transfers between devices, on_device(): lax.all_gather(out_share, 'col', axis=1, tiled=True)  18.8 us
    all_gather x1, waiting for transfers between devices, on_device(): lax.all_gather(cotangent, 'col', axis=1, tiled=True)  17 us
    all_gather x1, waiting for transfers between devices, on_device(): q_full = lax.all_gather(queries, 'col', axis=1, tiled=True)  16.3 us
  transfers between devices with their start and end apart: 9, of which 8 were waited for; matrix products, arithmetic and copies ran while one was open for 8% of the time, Pallas kernels for 0%

commit v1 on v0

--- a/solution.py
+++ b/solution.py
@@ -22,6 +22,27 @@
 
 
 def on_device(queries, keys, values, cotangent, block_lists, block_counts):
+
+    def convert_samples_all_all(arr):
+        z = lax.axis_size("col")
+        out_arr, next_value, frame_out = (z, lax.axis_index("col"), arr.shape[1])
+        y2, all_rows = (arr, 1)
+        while all_rows < out_arr:
+            y2 = jnp.concatenate(
+                [
+                    y2,
+                    lax.ppermute(
+                        y2,
+                        axis_name="col",
+                        perm=[(pp, (pp - all_rows) % out_arr) for pp in range(out_arr)],
+                    ),
+                ],
+                axis=1,
+            )
+            all_rows = 2 * all_rows
+        work_now = jnp.roll(y2, shift=next_value * frame_out, axis=1)
+        return work_now
+
     score_scale = 1.0 / math.sqrt(HEAD)
     q_full = lax.all_gather(queries, "col", axis=1, tiled=True)
     k_full, v_full = (
@@ -111,7 +132,7 @@
     )
     grad_full, out_full = (
         lax.all_gather(cotangent, "col", axis=1, tiled=True),
-        lax.all_gather(out_share, "col", axis=1, tiled=True),
+        convert_samples_all_all(out_share),
     )
     delta = jnp.einsum(
         "qhd,qhd->hq",

time: 405 us -> 398 us (0.983)
  waiting for transfers between devices: 223 us -> 211 us
    ppermute x0 -> x2, waiting for transfers between devices: none -> 21.4 us  [convert_samples_all_all(): lax.ppermute(y2, axis_name='col', perm=[(pp, (pp - all_rows) % out_arr) f...]
    all_gather x1 -> x0, waiting for transfers between devices: 18.8 us -> none  [on_device(): lax.all_gather(out_share, 'col', axis=1, tiled=True)]
    all_gather x1, waiting for transfers between devices: 17 us -> 0.01 us  [on_device(): lax.all_gather(cotangent, 'col', axis=1, tiled=True)]
    unnamed x23 -> x25, local copies, waits for them, and re-layouts: 12.4 us -> 14.4 us
  transfers between devices with their start and end apart: 9 -> 10, of which waited for: 8 -> 8; matrix products, arithmetic and copies ran while one was open for 8% -> 10% of each run, Pallas kernels for 0% -> 0%
where the time goes in v1:
time: 398 us; the launch traced here: 396 us
  waiting for transfers between devices  211 us (53%)
  local copies, waits for them, and re-layouts  57.1 us (14%)
  other arithmetic  41.1 us (10%)
  matrix products  40.3 us (10%)
  blocking collectives  21.5 us (5%)
  between operations  14.3 us (4%)
  loops' own time  8.56 us (2%)
    reduce_scatter x1, waiting for transfers between devices, on_device(): lax.psum_scatter(key_parts, 'row', scatter_dimension=1, tiled=True)  44.6 us
    reduce_scatter x1, waiting for transfers between devices, on_device(): lax.psum_scatter(value_parts, 'row', scatter_dimension=1, tiled=True)  37.9 us
    reduce_scatter x1, waiting for transfers between devices, on_device(): lax.psum_scatter(query_parts, 'col', scatter_dimension=1, tiled=True)  31.5 us
    all_gather x1, waiting for transfers between devices, on_device(): lax.all_gather(keys, 'row', axis=1, tiled=True)  30.1 us
    reduce_scatter x1, waiting for transfers between devices, on_device(): lax.psum_scatter(partial_out, 'col', scatter_dimension=1, tiled=True)  29.6 us
    ppermute x2, waiting for transfers between devices, convert_samples_all_all(): lax.ppermute(y2, axis_name='col', perm=[(pp, (pp - all_rows) % out_arr) f...  21.4 us
    all_gather x1, waiting for transfers between devices, on_device(): q_full = lax.all_gather(queries, 'col', axis=1, tiled=True)  16.3 us
    dot_general x4, matrix products, output_work(): jnp.einsum('hqk,khd->qhd', weights, value_heads, preferred_element_type=j...  15.3 us
  transfers between devices with their start and end apart: 10, of which 8 were waited for; matrix products, arithmetic and copies ran while one was open for 10% of the time, Pallas kernels for 0%

profile of v1, /device:TPU:0, one launch (start us, length us, event | category | flops | bytes accessed | tf_op | source)
XLA Modules:
  0.0 396.1 jit_solution(2193601332222021265)
XLA Ops:
  13.3 16.3 %all-gather.7.cloned.1.call-done = bf16[512,1024]{0,1:T(8,128)(2,1)} async-done(((bf16[512,256]{0,1:T(8,128)(2,1)}), bf16[512,1024]{0,1:T(8,128)(2,1)}) %all-gather.7.cloned.1.call-update) | async-done | bytes 1048592 | tf_op jit(solution)/shard_map/all_gather | solution.py:47
  29.6 30.1 %all-gather.5.cloned.1.call-done = bf16[512,1024]{0,1:T(8,128)(2,1)} async-done(((bf16[512,256]{0,1:T(8,128)(2,1)}), bf16[512,1024]{0,1:T(8,128)(2,1)}) %all-gather.5.cloned.1.call-update) | async-done | bytes 1048592 | tf_op jit(solution)/shard_map/all_gather | solution.py:49
  59.7 22.0 %while.57 = (s32[]{:T(128)}, f32[16,512]{1,0:T(8,128)S(1)}, f32[16,512]{1,0:T(8,128)S(1)}, pred[1,4]{1,0:T(4,128)(4,1)S(1)}, bf16[512,1024]{0,1:T(8,128)(2,1)}, ...) while((s32[]{:T(128)}, f32[16,512]{1,0:T(8,128)S(1)}, ...), condition=%wide.region_7.8_spmd.clone, body=%wide.region_2.7_spmd.clone.sunk | while | flops 142622736 | bytes 10658168 | solution.py:102
  60.4 4.8 %conditional.9 = ((f32[16,512]{1,0:T(8,128)S(1)}, f32[16,512]{1,0:T(8,128)S(1)})) conditional(s32[]{:T(128)} %bitcast.68, (f32[16,512]{1,0:T(8,128)S(1)}, f32[16,512]{1,0:T(8,128)S(1)}) %tuple.195, (pred[4,4]{1,0:T(4,128)(4,1)S(1)}, s32[]{:T(128)}, s32[]{:T(128)}, bf16[512,1024]{0,1:T(8,128)(2,1)}, bf16[512,1024]{0,1:T(8,128)(2,1)}, ...), branch_computations={%region_3.3_spmd, %region_4.6_spmd} | conditional | flops 142622720 | bytes 10657886 | solution.py:98
  65.9 4.9 %conditional.9 = ((f32[16,512]{1,0:T(8,128)S(1)}, f32[16,512]{1,0:T(8,128)S(1)})) conditional(s32[]{:T(128)} %bitcast.68, (f32[16,512]{1,0:T(8,128)S(1)}, f32[16,512]{1,0:T(8,128)S(1)}) %tuple.195, (pred[4,4]{1,0:T(4,128)(4,1)S(1)}, s32[]{:T(128)}, s32[]{:T(128)}, bf16[512,1024]{0,1:T(8,128)(2,1)}, bf16[512,1024]{0,1:T(8,128)(2,1)}, ...), branch_computations={%region_3.3_spmd, %region_4.6_spmd} | conditional | flops 142622720 | bytes 10657886 | solution.py:98
  71.4 4.8 %conditional.9 = ((f32[16,512]{1,0:T(8,128)S(1)}, f32[16,512]{1,0:T(8,128)S(1)})) conditional(s32[]{:T(128)} %bitcast.68, (f32[16,512]{1,0:T(8,128)S(1)}, f32[16,512]{1,0:T(8,128)S(1)}) %tuple.195, (pred[4,4]{1,0:T(4,128)(4,1)S(1)}, s32[]{:T(128)}, s32[]{:T(128)}, bf16[512,1024]{0,1:T(8,128)(2,1)}, bf16[512,1024]{0,1:T(8,128)(2,1)}, ...), branch_computations={%region_3.3_spmd, %region_4.6_spmd} | conditional | flops 142622720 | bytes 10657886 | solution.py:98
  76.9 4.8 %conditional.9 = ((f32[16,512]{1,0:T(8,128)S(1)}, f32[16,512]{1,0:T(8,128)S(1)})) conditional(s32[]{:T(128)} %bitcast.68, (f32[16,512]{1,0:T(8,128)S(1)}, f32[16,512]{1,0:T(8,128)S(1)}) %tuple.195, (pred[4,4]{1,0:T(4,128)(4,1)S(1)}, s32[]{:T(128)}, s32[]{:T(128)}, bf16[512,1024]{0,1:T(8,128)(2,1)}, bf16[512,1024]{0,1:T(8,128)(2,1)}, ...), branch_computations={%region_3.3_spmd, %region_4.6_spmd} | conditional | flops 142622720 | bytes 10657886 | solution.py:98
  81.8 11.3 %pmax.7 = bf16[16,512]{1,0:T(8,128)(2,1)S(1)} all-reduce(bf16[16,512]{1,0:T(8,128)(2,1)S(1)} %convert_element_type.89), channel_id=1, replica_groups=mesh['groups'=2,'row'=4,'col'=4] {'col'}, use_global_device_ids=true, to_apply=%region_8.9 | all-reduce | flops 8192 | bytes 32768 | tf_op jit(solution)/shard_map/pmax | solution.py:103
  93.1 10.3 %psum.7 = f32[16,512]{1,0:T(8,128)S(1)} all-reduce(f32[16,512]{1,0:T(8,128)S(1)} %exponential_multiply_fusion), channel_id=1, replica_groups=mesh['groups'=2,'row'=4,'col'=4] {'col'}, use_global_device_ids=true, to_apply=%region_9.10 | all-reduce | flops 8192 | bytes 65536 | tf_op jit(solution)/shard_map/psum | solution.py:104
  103.6 36.9 %while.58 = (s32[]{:T(128)}, f32[512,1024]{0,1:T(8,128)S(1)}, pred[1,4]{1,0:T(4,128)(4,1)S(1)}, bf16[512,1024]{0,1:T(8,128)(2,1)}, bf16[512,1024]{0,1:T(8,128)(2...) while((s32[]{:T(128)}, f32[512,1024]{0,1:T(8,128)S(1)}, ...), condition=%wide.region_13.14_spmd.clone, body=%wide.region_10.13_spmd.clone.sunk | while | flops 275251200 | bytes 11083640 | solution.py:129
  104.3 8.6 %conditional.10 = (f32[512,1024]{0,1:T(8,128)S(1)}) conditional(s32[]{:T(128)} %bitcast.69, f32[512,1024]{0,1:T(8,128)S(1)} %get-tuple-element.1619, (pred[4,4]{1,0:T(4,128)(4,1)S(1)}, s32[]{:T(128)}, s32[]{:T(128)}, bf16[512,1024]{0,1:T(8,128)(2,1)}, bf16[512,1024]{0,1:T(8,128)(2,1)S(1)}, /*index=5*/f32[16,512]{1,0:T(8,128)S(1)}, ...), branch_computations={%region_11.11_spmd, %region_12.12_spmd} | conditional | flops 275251200 | bytes 11083342 | solution.py:127
  106.9 3.8 fusion.9
  113.5 8.6 %conditional.10 = (f32[512,1024]{0,1:T(8,128)S(1)}) conditional(s32[]{:T(128)} %bitcast.69, f32[512,1024]{0,1:T(8,128)S(1)} %get-tuple-element.1619, (pred[4,4]{1,0:T(4,128)(4,1)S(1)}, s32[]{:T(128)}, s32[]{:T(128)}, bf16[512,1024]{0,1:T(8,128)(2,1)}, bf16[512,1024]{0,1:T(8,128)(2,1)S(1)}, /*index=5*/f32[16,512]{1,0:T(8,128)S(1)}, ...), branch_computations={%region_11.11_spmd, %region_12.12_spmd} | conditional | flops 275251200 | bytes 11083342 | solution.py:127
  116.1 3.8 fusion.9
  122.8 8.6 %conditional.10 = (f32[512,1024]{0,1:T(8,128)S(1)}) conditional(s32[]{:T(128)} %bitcast.69, f32[512,1024]{0,1:T(8,128)S(1)} %get-tuple-element.1619, (pred[4,4]{1,0:T(4,128)(4,1)S(1)}, s32[]{:T(128)}, s32[]{:T(128)}, bf16[512,1024]{0,1:T(8,128)(2,1)}, bf16[512,1024]{0,1:T(8,128)(2,1)S(1)}, /*index=5*/f32[16,512]{1,0:T(8,128)S(1)}, ...), branch_computations={%region_11.11_spmd, %region_12.12_spmd} | conditional | flops 275251200 | bytes 11083342 | solution.py:127
  125.3 3.8 fusion.9
  132.0 8.6 %conditional.10 = (f32[512,1024]{0,1:T(8,128)S(1)}) conditional(s32[]{:T(128)} %bitcast.69, f32[512,1024]{0,1:T(8,128)S(1)} %get-tuple-element.1619, (pred[4,4]{1,0:T(4,128)(4,1)S(1)}, s32[]{:T(128)}, s32[]{:T(128)}, bf16[512,1024]{0,1:T(8,128)(2,1)}, bf16[512,1024]{0,1:T(8,128)(2,1)S(1)}, /*index=5*/f32[16,512]{1,0:T(8,128)S(1)}, ...), branch_computations={%region_11.11_spmd, %region_12.12_spmd} | conditional | flops 275251200 | bytes 11083342 | solution.py:127
  134.6 3.8 fusion.9
  142.9 29.6 %reduce-scatter.5.cloned.1.call-done = f32[512,256]{0,1:T(8,128)} async-done(((f32[512,1024]{0,1:T(8,128)}), f32[512,256]{0,1:T(8,128)}) %reduce-scatter.5.cloned.1.call-update) | async-done | bytes 524304 | tf_op jit(solution)/shard_map/reduce_scatter | solution.py:130
  174.2 3.9 collective-permute-done
  180.4 17.5 %collective-permute-done.1 = bf16[512,512]{0,1:T(8,128)(2,1)S(1)} collective-permute-done((bf16[512,512]{0,1:T(8,128)(2,1)S(1)}, bf16[512,512]{0,1:T(8,128)(2,1)S(1)}, u32[]{:S(2)}, u32[]{:S(2)}) %collective-permute-start.1) | collective-permute-done | bytes 524320 | tf_op jit(solution)/shard_map/ppermute | solution.py:34
  207.7 51.7 %while.59 = (s32[]{:T(128)}, f32[512,1024]{0,1:T(8,128)}, f32[512,1024]{0,1:T(8,128)}, f32[512,1024]{0,1:T(8,128)}, pred[1,4]{1,0:T(4,128)(4,1)S(1)}, /*index=5*...) while((s32[]{:T(128)}, f32[512,1024]{0,1:T(8,128)}, ...), condition=%wide.region_18.19_spmd.clone, body=%wide.region_15.18_spmd.clone.sunk | while | flops 683016192 | bytes 48078884 | solution.py:194
  208.2 12.3 %conditional.11 = ((f32[512,1024]{0,1:T(8,128)}, f32[512,1024]{0,1:T(8,128)}, f32[512,1024]{0,1:T(8,128)})) conditional(s32[]{:T(128)} %bitcast.70, (f32[512,1024]{0,1:T(8,128)}, f32[512,1024]{0,1:T(8,128)}, f32[512,1024]{0,1:T(8,128)}) %tuple.200, (pred[4,4]{1,0:T(4,128)(4,1)S(1)}, s32[]{:T(128)}, s32[]{:T(128)}, bf16[512,1024]{0,1:T(8,128)(2,1)}, ...), branch_computations={%region_16.16_spmd, %region_17.17_spmd} | conditional | flops 683016192 | bytes 48078500 | solution.py:187
  221.2 12.4 %conditional.11 = ((f32[512,1024]{0,1:T(8,128)}, f32[512,1024]{0,1:T(8,128)}, f32[512,1024]{0,1:T(8,128)})) conditional(s32[]{:T(128)} %bitcast.70, (f32[512,1024]{0,1:T(8,128)}, f32[512,1024]{0,1:T(8,128)}, f32[512,1024]{0,1:T(8,128)}) %tuple.200, (pred[4,4]{1,0:T(4,128)(4,1)S(1)}, s32[]{:T(128)}, s32[]{:T(128)}, bf16[512,1024]{0,1:T(8,128)(2,1)}, ...), branch_computations={%region_16.16_spmd, %region_17.17_spmd} | conditional | flops 683016192 | bytes 48078500 | solution.py:187
  231.2 2.4 constant_dynamic-update-slice_fusion
  234.1 12.3 %conditional.11 = ((f32[512,1024]{0,1:T(8,128)}, f32[512,1024]{0,1:T(8,128)}, f32[512,1024]{0,1:T(8,128)})) conditional(s32[]{:T(128)} %bitcast.70, (f32[512,1024]{0,1:T(8,128)}, f32[512,1024]{0,1:T(8,128)}, f32[512,1024]{0,1:T(8,128)}) %tuple.200, (pred[4,4]{1,0:T(4,128)(4,1)S(1)}, s32[]{:T(128)}, s32[]{:T(128)}, bf16[512,1024]{0,1:T(8,128)(2,1)}, ...), branch_computations={%region_16.16_spmd, %region_17.17_spmd} | conditional | flops 683016192 | bytes 48078500 | solution.py:187
  247.0 12.4 %conditional.11 = ((f32[512,1024]{0,1:T(8,128)}, f32[512,1024]{0,1:T(8,128)}, f32[512,1024]{0,1:T(8,128)})) conditional(s32[]{:T(128)} %bitcast.70, (f32[512,1024]{0,1:T(8,128)}, f32[512,1024]{0,1:T(8,128)}, f32[512,1024]{0,1:T(8,128)}) %tuple.200, (pred[4,4]{1,0:T(4,128)(4,1)S(1)}, s32[]{:T(128)}, s32[]{:T(128)}, bf16[512,1024]{0,1:T(8,128)(2,1)}, ...), branch_computations={%region_16.16_spmd, %region_17.17_spmd} | conditional | flops 683016192 | bytes 48078500 | solution.py:187
  257.0 2.4 constant_dynamic-update-slice_fusion
  259.4 2.9 copy.37
  270.0 37.9 %reduce-scatter.11.cloned.1.call-done = f32[512,256]{1,0:T(8,128)} async-done(((f32[512,1024]{1,0:T(8,128)}), f32[512,256]{1,0:T(8,128)}) %reduce-scatter.11.cloned.1.call-update) | async-done | bytes 524304 | tf_op jit(solution)/shard_map/reduce_scatter | solution.py:200
  309.7 31.5 %reduce-scatter.7.cloned.1.call-done = f32[512,256]{1,0:T(8,128)} async-done(((f32[512,1024]{1,0:T(8,128)}), f32[512,256]{1,0:T(8,128)}) %reduce-scatter.7.cloned.1.call-update) | async-done | bytes 524304 | tf_op jit(solution)/shard_map/reduce_scatter | solution.py:195
  343.0 44.6 %reduce-scatter.9.cloned.1.call-done = f32[512,256]{1,0:T(8,128)} async-done(((f32[512,1024]{1,0:T(8,128)}), f32[512,256]{1,0:T(8,128)}) %reduce-scatter.9.cloned.1.call-update) | async-done | bytes 524304 | tf_op jit(solution)/shard_map/reduce_scatter | solution.py:199
  (197 shorter events, 117.5 us)
Async XLA Ops:
  7.2 5.7 %copy-start.9 = (s32[4]{0:T(128)S(1)}, s32[4]{0:T(128)}, u32[]{:S(2)}) copy-start(s32[4]{0:T(128)} %param.23) | copy-start | bytes 52
  7.2 5.8 %copy-start.8 = (s32[4,16]{1,0:T(4,128)S(1)}, s32[4,16]{1,0:T(4,128)}, u32[]{:S(2)}) copy-start(s32[4,16]{1,0:T(4,128)} %param.22) | copy-start | bytes 772
  7.2 22.4 %all-gather.7.cloned.1.call-start = ((), (), s32[]{:S(2)}) async-start(), calls=%async_computation.5 | async-start | bytes 1310720 | tf_op jit(solution)/shard_map/all_gather | solution.py:47
  9.1 50.7 %all-gather.5.cloned.1.call-start = ((), (), s32[]{:S(2)}) async-start(), calls=%async_computation.4 | async-start | bytes 1310720 | tf_op jit(solution)/shard_map/all_gather | solution.py:49
  10.9 92.4 %all-gather.9.cloned.1.call-start = ((), (), s32[]{:S(2)}) async-start(), calls=%async_computation.6 | async-start | bytes 1310720 | tf_op jit(solution)/shard_map/all_gather | solution.py:50
  12.8 159.7 %reduce-scatter.5.cloned.1.call-start = ((), (), s32[]{:S(2)}) async-start(), calls=%async_computation.7 | async-start | bytes 2621440 | tf_op jit(solution)/shard_map/reduce_scatter | solution.py:130
  81.8 21.9 %copy-start.1 = (bf16[512,1024]{0,1:T(8,128)(2,1)S(1)}, bf16[512,1024]{0,1:T(8,128)(2,1)}, u32[]{:S(2)}) copy-start(bf16[512,1024]{0,1:T(8,128)(2,1)} %get-tuple-element.1708) | copy-start | bytes 3145732
  140.6 1.3 copy-start.5
  140.6 1.4 copy-start.7
  141.9 59.1 %all-gather.11.cloned.1.call-start = ((), (), s32[]{:S(2)}) async-start(), calls=%async_computation.8 | async-start | bytes 1310720 | tf_op jit(solution)/shard_map/all_gather | solution.py:134
  142.8 165.1 %reduce-scatter.11.cloned.1.call-start = ((), (), s32[]{:S(2)}) async-start(), calls=%async_computation.11 | async-start | bytes 2621440 | tf_op jit(solution)/shard_map/reduce_scatter | solution.py:200
  174.2 3.9 collective-permute-start
  178.2 19.7 %collective-permute-start.1 = (bf16[512,512]{0,1:T(8,128)(2,1)S(1)}, bf16[512,512]{0,1:T(8,128)(2,1)S(1)}, u32[]{:S(2)}, u32[]{:S(2)}) collective-permute-start(bf16[512,512]{0,1:T(8,128)(2,1)S(1)} %pad_maximum_fusion), channel_id=1, source_target_pairs={{0,2},{1,3},{2,0},{3,1},{4,6},{5,7},{6,4},{7,5},{8,10},{9,11},{10,... | collective-permute-start | bytes 1572872 | tf_op jit(solution)/shard_map/ppermute | solution.py:34
  204.5 3.2 copy-start
  214.8 1.6 copy-start.2
  216.9 1.3 copy-start.3
  227.7 1.6 copy-start.2
  229.8 1.3 copy-start.3
  240.7 1.6 copy-start.2
  242.8 1.3 copy-start.3
  253.6 1.6 copy-start.2
  255.7 1.3 copy-start.3
  262.3 1.6 copy-start.4
  262.4 78.8 %reduce-scatter.7.cloned.1.call-start = ((), (), s32[]{:S(2)}) async-start(), calls=%async_computation.9 | async-start | bytes 2621440 | tf_op jit(solution)/shard_map/reduce_scatter | solution.py:195
  265.8 1.6 copy-start.6
  265.8 121.7 %reduce-scatter.9.cloned.1.call-start = ((), (), s32[]{:S(2)}) async-start(), calls=%async_computation.10 | async-start | bytes 2621440 | tf_op jit(solution)/shard_map/reduce_scatter | solution.py:199
Sparse Core Ops, SparseCore 0:
  10.2 19.4 all-gather.6
  31.7 27.9 all-gather.4
  61.9 27.4 all-gather.8
  142.0 30.3 reduce-scatter.4
  174.5 22.4 all-gather.10
  262.5 45.3 reduce-scatter.10
  310.4 30.7 reduce-scatter.6
  343.6 43.8 reduce-scatter.8
